TPU v7x, 256 devices: a whole 4x4x8 slice. The times are simulated.
256 devices in a mesh: section: 8 (over y_hi, x), ctx: 32 (over y_lo, z, core).
Axes of the slice: x: 4, y: 4 (y_hi: 2, y_lo: 2; y = y_hi * 2 + y_lo), z: 8, core: 2. Of those that a mesh axis runs over, the one named last changes fastest.
Arguments:
- projected: bfloat16 [8, 12288, 3072], P('section', 'ctx'), may hold values from -64 to 64
- grad_out: bfloat16 [8, 12288, 3072], P('section', 'ctx'), may hold values from -6 to 6
- doc_lengths: int32 [31], replicated, may hold values from 1 to 768, as said below
Outputs:
- grad_kv: float32 [12288, 2048], P('ctx')
Inputs may be any that keep to these rules, and one draw needn't show every extreme that they name: `doc_lengths`: the lengths sum to 12288; the first document is shorter than 384 tokens and the second has exactly 768.
All inputs are finite; a program needn't handle non-finite values.
Results may differ from a plain program's by a relative error of at most 0.0031.
Values may be sent and summed in bfloat16 or wider, within the bound.
No kernel may reach another device: no remote copies, remote signals or barrier semaphores. Data moves between devices by JAX's collectives and lax.ppermute only.
A program may use at most 128 MiB of HBM per device.

v0:
```python
import math
import jax
import jax.numpy as jnp
from jax import lax
from jax.sharding import PartitionSpec as P

HEAD_SIZE = 128
KV_HEAD_COUNT = 8
QUERY_PER_KV = 3
REACH = 2
MASKED_SCORE = -1e30


def spread(value, axis, source):
    kept = jnp.where(lax.axis_index(axis) == source, value, 0).astype(value.dtype)
    return lax.psum(kept, axis)


def shifted(value, axis, steps):
    count = lax.axis_size(axis)
    leading, last = (max(0, -steps), min(count, count - steps))
    return lax.ppermute(value, axis, [(source, source + steps) for source in range(leading, last)])


def document_of(places, doc_ends):
    return jnp.sum((doc_ends[None, :] <= places[:, None]).astype(jnp.int32), axis=1)


def piece_scores(query_group, key_part, piece_mask, score_scale):
    scores = (
        jnp.einsum("qah,kh->aqk", query_group, key_part, preferred_element_type=jnp.float32)
        * score_scale
    )
    return jnp.where(piece_mask[None], scores, MASKED_SCORE)


def piece_attend(weight_part, value_part):
    return jnp.einsum("aqk,kh->qah", weight_part, value_part, preferred_element_type=jnp.float32)


def piece_grads(
    prob_part, weight_part, query_group, grad_group, value_part, delta_rows, score_scale
):
    grad_value = jnp.einsum(
        "aqk,qah->kh", weight_part, grad_group, preferred_element_type=jnp.float32
    )
    grad_prob = jnp.einsum(
        "qah,kh->aqk", grad_group, value_part, preferred_element_type=jnp.float32
    )
    grad_score = (prob_part * (grad_prob - delta_rows)).astype(jnp.bfloat16)
    grad_key = (
        jnp.einsum("aqk,qah->kh", grad_score, query_group, preferred_element_type=jnp.float32)
        * score_scale
    )
    return (grad_key, grad_value)


def on_device(projected, grad_out, doc_lengths):
    tok_rows = projected.shape[1]
    head_dim = HEAD_SIZE
    shared_key_heads = KV_HEAD_COUNT
    group = QUERY_PER_KV
    shared_width = shared_key_heads * head_dim
    out_width = 2 * shared_width
    reaching = REACH
    pieces = reaching + 1
    score_scale = 1.0 / math.sqrt(head_dim)
    shared = spread(projected[0][:, :out_width], "section", 0)
    earlier = []
    for distance in range(reaching, 0, -1):
        earlier.append(shifted(shared, "ctx", distance))
    window = jnp.concatenate(earlier + [shared], axis=0)
    key_heads = window[:, :shared_width].reshape(pieces * tok_rows, shared_key_heads, head_dim)
    value_heads = window[:, shared_width:].reshape(pieces * tok_rows, shared_key_heads, head_dim)
    queries = projected[0].reshape(tok_rows, shared_key_heads, group, head_dim)
    grad_heads = grad_out[0].reshape(tok_rows, shared_key_heads, group, head_dim)
    doc_ends = jnp.cumsum(doc_lengths)
    ctx_index = lax.axis_index("ctx")
    query_place = ctx_index * tok_rows + jnp.arange(tok_rows, dtype=jnp.int32)
    key_place = (ctx_index - reaching) * tok_rows + jnp.arange(pieces * tok_rows, dtype=jnp.int32)
    same_doc = (
        document_of(query_place, doc_ends)[:, None] == document_of(key_place, doc_ends)[None, :]
    )
    allowed = same_doc & (key_place[None, :] <= query_place[:, None]) & (key_place[None, :] >= 0)

    def group_grads(kv_index):
        query_group = lax.dynamic_index_in_dim(queries, kv_index, 1, keepdims=False)
        grad_group = lax.dynamic_index_in_dim(grad_heads, kv_index, 1, keepdims=False)
        key_group = lax.dynamic_index_in_dim(key_heads, kv_index, 1, keepdims=False)
        value_group = lax.dynamic_index_in_dim(value_heads, kv_index, 1, keepdims=False)
        score_parts = []
        for index in range(pieces):
            rows = slice(index * tok_rows, (index + 1) * tok_rows)
            score_parts.append(
                piece_scores(query_group, key_group[rows], allowed[:, rows], score_scale)
            )
        scores = jnp.concatenate(score_parts, axis=2)
        row_top = jnp.max(scores, axis=2, keepdims=True)
        powers = jnp.exp(scores - row_top)
        attn_weight = powers / jnp.sum(powers, axis=2, keepdims=True)
        attn_half = attn_weight.astype(jnp.bfloat16)
        attended = jnp.zeros((tok_rows, group, head_dim), jnp.float32)
        for index in range(pieces):
            rows = slice(index * tok_rows, (index + 1) * tok_rows)
            attended = attended + piece_attend(attn_half[:, :, rows], value_group[rows])
        delta_rows = jnp.sum(grad_group.astype(jnp.float32) * attended, axis=2).T[:, :, None]
        key_parts = []
        value_parts = []
        for index in range(pieces):
            rows = slice(index * tok_rows, (index + 1) * tok_rows)
            grad_key, grad_value = piece_grads(
                attn_weight[:, :, rows],
                attn_half[:, :, rows],
                query_group,
                grad_group,
                value_group[rows],
                delta_rows,
                score_scale,
            )
            key_parts.append(grad_key)
            value_parts.append(grad_value)
        return (jnp.concatenate(key_parts, axis=0), jnp.concatenate(value_parts, axis=0))

    key_grads, value_grads = lax.map(group_grads, jnp.arange(shared_key_heads, dtype=jnp.int32))
    is_cross = (lax.axis_index("section") > 0).astype(jnp.float32)
    key_flat = jnp.transpose(key_grads, (1, 0, 2)).reshape(pieces * tok_rows, shared_width)
    value_flat = jnp.transpose(value_grads, (1, 0, 2)).reshape(pieces * tok_rows, shared_width)
    grad_pieces = (jnp.concatenate([key_flat, value_flat], axis=1) * is_cross).reshape(
        pieces, tok_rows, out_width
    )
    summed = grad_pieces[reaching]
    for distance in range(1, reaching + 1):
        summed = summed + shifted(grad_pieces[reaching - distance], "ctx", -distance)
    return lax.psum(summed, "section")


def solution(mesh):
    return jax.shard_map(
        on_device,
        mesh=mesh,
        in_specs=(P("section", "ctx", None), P("section", "ctx", None), P()),
        out_specs=P("ctx", None),
        check_vma=False,
    )
```

profile of v0, /device:TPU:32, one launch (start us, length us, event | category | flops | bytes accessed | tf_op | source)
XLA Modules:
  0.0 628.3 jit_solution(13634412280099903388)
XLA Ops:
  6.5 4.3 copy.56
  10.8 2.9 slice_select_fusion
  13.8 97.9 %all-reduce.3.cloned.1.call-done = bf16[384,2048]{0,1:T(8,128)(2,1)} async-done(((bf16[384,2048]{0,1:T(8,128)(2,1)}), bf16[384,2048]{0,1:T(8,128)(2,1)}) %all-reduce.3.cloned.1.call-update) | async-done | bytes 1572880 | tf_op jit(solution)/shard_map/psum | solution.py:16
  111.6 3.5 collective-permute-start
  115.1 1.9 collective-permute-start.1
  117.3 2.4 copy.58
  120.0 2.0 and_and_fusion
  122.0 29.1 %collective-permute-done = bf16[384,2048]{0,1:T(8,128)(2,1)} collective-permute-done((bf16[384,2048]{0,1:T(8,128)(2,1)}, bf16[384,2048]{0,1:T(8,128)(2,1)}, u32[]{:S(2)}, u32[]{:S(2)}) %collective-permute-start) | collective-permute-done | bytes 1572896 | tf_op jit(solution)/shard_map/ppermute | solution.py:22
  151.1 1.6 constant_dynamic-update-slice_fusion.2
  152.7 8.9 %collective-permute-done.1 = bf16[384,2048]{0,1:T(8,128)(2,1)} collective-permute-done((bf16[384,2048]{0,1:T(8,128)(2,1)}, bf16[384,2048]{0,1:T(8,128)(2,1)}, u32[]{:S(2)}, u32[]{:S(2)}) %collective-permute-start.1) | collective-permute-done | bytes 1572896 | tf_op jit(solution)/shard_map/ppermute | solution.py:22
  161.5 1.7 constant_dynamic-update-slice_fusion.1
  163.6 2.5 fusion.71
  166.1 224.7 %while.12 = (s32[]{:T(128)}, f32[8,1152,128]{2,1,0:T(8,128)}, f32[8,1152,128]{2,1,0:T(8,128)}, pred[384,1152]{0,1:T(8,128)(4,1)}, s32[8]{0:T(128)S(1)}, /*index=...) while((s32[]{:T(128)}, f32[8,1152,128]{2,1,0:T(8,128)}, ...), condition=%wide.region_10.11_spmd, body=%wide.region_4.10_spmd.sunk | while | flops 1720070784 | bytes 68940056 | solution.py:124
  169.8 1.5 fusion.117
  175.2 3.7 fusion.121
  183.0 1.9 fusion.123
  184.9 2.3 fusion.126
  187.2 2.4 fusion.125
  189.6 2.3 fusion.124
  203.3 3.7 fusion.121
  211.1 1.9 fusion.123
  212.9 2.3 fusion.126
  215.2 2.4 fusion.125
  217.7 2.3 fusion.124
  231.3 3.7 fusion.121
  239.1 1.9 fusion.123
  241.0 2.3 fusion.126
  243.3 2.4 fusion.125
  245.8 2.3 fusion.124
  259.5 3.7 fusion.121
  267.3 1.9 fusion.123
  269.2 2.3 fusion.126
  271.4 2.4 fusion.125
  273.9 2.3 fusion.124
  283.7 1.5 fusion.118
  287.5 3.7 fusion.121
  295.3 1.9 fusion.123
  297.2 2.3 fusion.126
  299.5 2.4 fusion.125
  301.9 2.3 fusion.124
  315.6 3.7 fusion.121
  323.4 1.9 fusion.123
  325.3 2.3 fusion.126
  327.6 2.4 fusion.125
  330.0 2.3 fusion.124
  343.7 3.7 fusion.121
  351.5 1.9 fusion.123
  353.4 2.3 fusion.126
  355.7 2.4 fusion.125
  358.1 2.3 fusion.124
  371.8 3.7 fusion.121
  379.6 1.9 fusion.123
  381.5 2.3 fusion.126
  383.8 2.4 fusion.125
  386.2 2.3 fusion.124
  390.8 8.7 %copy_bitcast_fusion = (f32[1152,1024]{1,0:T(8,128)}, f32[1152,1024]{1,0:T(8,128)}) fusion(f32[8,1152,128]{2,1,0:T(8,128)} %get-tuple-element.53, f32[8,1152,128]{2,1,0:T(8,128)} %get-tuple-element.54), kind=kLoop, calls=%fused_computation.83 | loop fusion | bytes 18874368 | tf_op jit(solution)/shard_map/reshape | solution.py:127
  399.5 4.9 maximum_multiply_fusion
  405.1 1.9 collective-permute-start.2
  407.0 1.9 collective-permute-start.3
  409.0 64.8 %collective-permute-done.2 = f32[384,2048]{1,0:T(8,128)S(1)} collective-permute-done((f32[384,2048]{1,0:T(8,128)S(1)}, f32[384,2048]{1,0:T(8,128)S(1)}, u32[]{:S(2)}, u32[]{:S(2)}) %collective-permute-start.2) | collective-permute-done | bytes 3145760 | tf_op jit(solution)/shard_map/ppermute | solution.py:22
  473.8 37.5 %collective-permute-done.3 = f32[384,2048]{1,0:T(8,128)S(1)} collective-permute-done((f32[384,2048]{1,0:T(8,128)S(1)}, f32[384,2048]{1,0:T(8,128)S(1)}, u32[]{:S(2)}, u32[]{:S(2)}) %collective-permute-start.3) | collective-permute-done | bytes 3145760 | tf_op jit(solution)/shard_map/ppermute | solution.py:22
  511.2 2.7 fusion.63
  513.9 103.6 %all-reduce.5.cloned.1.call-done = f32[384,2048]{1,0:T(8,128)} async-done(((f32[384,2048]{1,0:T(8,128)}), f32[384,2048]{1,0:T(8,128)}) %all-reduce.5.cloned.1.call-update) | async-done | bytes 3145744 | tf_op jit(solution)/shard_map/psum | solution.py:134
  617.5 3.9 copy.108
  (173 shorter events, 106.4 us)
Async XLA Ops:
  6.5 105.1 %all-reduce.3.cloned.1.call-start = ((), (), s32[]{:S(2)}) async-start(), calls=%async_computation | async-start | bytes 3145728 | tf_op jit(solution)/shard_map/psum | solution.py:16
  10.8 106.2 %copy-start.4 = (s32[31]{0:T(128)S(1)}, s32[31]{0:T(128)}, u32[]{:S(2)}) copy-start(s32[31]{0:T(128)} %param.7) | copy-start | bytes 376
  10.8 106.5 %copy-start.2 = (bf16[1,384,3072]{2,1,0:T(8,128)(2,1)S(1)}, bf16[1,384,3072]{2,1,0:T(8,128)(2,1)}, u32[]{:S(2)}) copy-start(bf16[1,384,3072]{2,1,0:T(8,128)(2,1)} %param.6) | copy-start | bytes 7077892
  13.7 603.8 %all-reduce.5.cloned.1.call-start = ((), (), s32[]{:S(2)}) async-start(), calls=%async_computation.1 | async-start | bytes 6291456 | tf_op jit(solution)/shard_map/psum | solution.py:134
  111.6 39.5 %collective-permute-start = (bf16[384,2048]{0,1:T(8,128)(2,1)}, bf16[384,2048]{0,1:T(8,128)(2,1)}, u32[]{:S(2)}, u32[]{:S(2)}) collective-permute-start(bf16[384,2048]{0,1:T(8,128)(2,1)} %all-reduce.3.cloned.1.call-done), channel_id=1, source_target_pairs={{0,2},{1,3},{2,4},{3,5},{4,6},{5,7},{6,8},{7,9},{8,10},{9,11},{10,... | collective-permute-start | bytes 4718600 | tf_op jit(solution)/shard_map/ppermute | solution.py:22
  115.1 46.4 %collective-permute-start.1 = (bf16[384,2048]{0,1:T(8,128)(2,1)}, bf16[384,2048]{0,1:T(8,128)(2,1)}, u32[]{:S(2)}, u32[]{:S(2)}) collective-permute-start(bf16[384,2048]{0,1:T(8,128)(2,1)} %all-reduce.3.cloned.1.call-done), channel_id=1, source_target_pairs={{0,1},{1,2},{2,3},{3,4},{4,5},{5,6},{6,7},{7,8},{8,9},{9,10},{10,1... | collective-permute-start | bytes 4718600 | tf_op jit(solution)/shard_map/ppermute | solution.py:22
  122.0 41.2 %copy-start.3 = (bf16[384,2048]{0,1:T(8,128)(2,1)S(1)}, bf16[384,2048]{0,1:T(8,128)(2,1)}, u32[]{:S(2)}) copy-start(bf16[384,2048]{0,1:T(8,128)(2,1)} %all-reduce.3.cloned.1.call-done) | copy-start | bytes 4718596
  178.9 1.5 copy-start
  187.2 4.7 copy-start.1
  207.0 1.5 copy-start
  215.2 4.7 copy-start.1
  235.0 1.5 copy-start
  243.3 4.7 copy-start.1
  263.2 1.5 copy-start
  271.4 4.7 copy-start.1
  291.2 1.5 copy-start
  299.5 4.7 copy-start.1
  319.3 1.5 copy-start
  327.6 4.7 copy-start.1
  347.4 1.5 copy-start
  355.7 4.7 copy-start.1
  375.5 1.5 copy-start
  383.8 4.7 copy-start.1
  405.1 68.7 %collective-permute-start.2 = (f32[384,2048]{1,0:T(8,128)S(1)}, f32[384,2048]{1,0:T(8,128)S(1)}, u32[]{:S(2)}, u32[]{:S(2)}) collective-permute-start(f32[384,2048]{1,0:T(8,128)S(1)} %get-tuple-element.113), channel_id=1, source_target_pairs={{1,0},{2,1},{3,2},{4,3},{5,4},{6,5},{7,6},{8,7},{9,8},{10,9},{11,1... | collective-permute-start | bytes 9437192 | tf_op jit(solution)/shard_map/ppermute | solution.py:22
  407.0 104.2 %collective-permute-start.3 = (f32[384,2048]{1,0:T(8,128)S(1)}, f32[384,2048]{1,0:T(8,128)S(1)}, u32[]{:S(2)}, u32[]{:S(2)}) collective-permute-start(f32[384,2048]{1,0:T(8,128)S(1)} %get-tuple-element.114), channel_id=1, source_target_pairs={{2,0},{3,1},{4,2},{5,3},{6,4},{7,5},{8,6},{9,7},{10,8},{11,9},{12,... | collective-permute-start | bytes 9437192 | tf_op jit(solution)/shard_map/ppermute | solution.py:22
Sparse Core Ops, SparseCore 0:
  13.8 97.7 all-reduce.2
  514.1 103.3 all-reduce.4
where the time goes:
time: 631 us; the launch traced here: 628 us
  waiting for transfers between devices  342 us (54%)
  matrix products  140 us (22%)
  other arithmetic  57.2 us (9%)
  local copies, waits for them, and re-layouts  50.6 us (8%)
  loops' own time  16.4 us (3%)
  between operations  13.5 us (2%)
  starting transfers between devices  9.26 us (1%)
    ppermute x4, waiting for transfers between devices, shifted(): lax.ppermute(value, axis, [(source, source + steps) for source in range(l...  140 us
    psum x1, waiting for transfers between devices, on_device(): return lax.psum(summed, 'section')  104 us
    psum x1, waiting for transfers between devices, spread(): return lax.psum(kept, axis)  97.9 us
    dot_general x24, matrix products, piece_grads(): jnp.einsum('aqk,qah->kh', grad_score, query_group, preferred_element_type...  55.7 us
    dot_general x24, matrix products, piece_attend(): jnp.einsum('aqk,kh->qah', weight_part, value_part, preferred_element_type...  37.8 us
    dot_general x24, matrix products, piece_scores(): jnp.einsum('qah,kh->aqk', query_group, key_part, preferred_element_type=j...  36.8 us
    convert_element_type x8, other arithmetic, group_grads(): attn_half = attn_weight.astype(jnp.bfloat16)  29.6 us
    another operation x1, loops' own time, on_device(): lax.map(group_grads, jnp.arange(shared_key_heads, dtype=jnp.int32))  16.4 us
  transfers between devices with their start and end apart: 6, of which 6 were waited for; matrix products, arithmetic and copies ran while one was open for 1% of the time, Pallas kernels for 0%

commit v1 on v0

--- a/solution.py
+++ b/solution.py
@@ -3,6 +3,7 @@
 import jax.numpy as jnp
 from jax import lax
 from jax.sharding import PartitionSpec as P
+from jax.lax import all_gather
 
 HEAD_SIZE = 128
 KV_HEAD_COUNT = 8
@@ -13,7 +14,7 @@
 
 def spread(value, axis, source):
     kept = jnp.where(lax.axis_index(axis) == source, value, 0).astype(value.dtype)
-    return lax.psum(kept, axis)
+    return all_gather(kept, axis).sum(axis=0)
 
 
 def shifted(value, axis, steps):

time: 631 us -> 699 us (1.11)
  waiting for transfers between devices: 342 us -> 400 us
  other arithmetic: 57.2 us -> 68.3 us
    all_gather x0 -> x1, waiting for transfers between devices: none -> 155 us  [spread(): return all_gather(kept, axis).sum(axis=0)]
    psum x1 -> x0, waiting for transfers between devices: 97.9 us -> none  [spread(): return lax.psum(kept, axis)]
    reduce_sum x0 -> x1, other arithmetic: none -> 9.2 us  [spread(): return all_gather(kept, axis).sum(axis=0)]
where the time goes in v1:
time: 699 us; the launch traced here: 696 us
  waiting for transfers between devices  400 us (57%)
  matrix products  139 us (20%)
  other arithmetic  68.3 us (10%)
  local copies, waits for them, and re-layouts  49.9 us (7%)
  loops' own time  16.4 us (2%)
  between operations  13.5 us (2%)
  starting transfers between devices  9.57 us (1%)
    all_gather x1, waiting for transfers between devices, spread(): return all_gather(kept, axis).sum(axis=0)  155 us
    ppermute x4, waiting for transfers between devices, shifted(): lax.ppermute(value, axis, [(source, source + steps) for source in range(l...  142 us
    psum x1, waiting for transfers between devices, on_device(): return lax.psum(summed, 'section')  103 us
    dot_general x24, matrix products, piece_grads(): jnp.einsum('aqk,qah->kh', grad_score, query_group, preferred_element_type...  54.8 us
    dot_general x24, matrix products, piece_attend(): jnp.einsum('aqk,kh->qah', weight_part, value_part, preferred_element_type...  37.9 us
    dot_general x24, matrix products, piece_scores(): jnp.einsum('qah,kh->aqk', query_group, key_part, preferred_element_type=j...  36.8 us
    convert_element_type x8, other arithmetic, group_grads(): attn_half = attn_weight.astype(jnp.bfloat16)  29.6 us
    another operation x1, loops' own time, on_device(): lax.map(group_grads, jnp.arange(shared_key_heads, dtype=jnp.int32))  16.4 us
  transfers between devices with their start and end apart: 6, of which 6 were waited for; matrix products, arithmetic and copies ran while one was open for 1% of the time, Pallas kernels for 0%

profile of v1, /device:TPU:32, one launch (start us, length us, event | category | flops | bytes accessed | tf_op | source)
XLA Modules:
  0.0 696.4 jit_solution(5229840966965574186)
XLA Ops:
  6.5 2.7 slice_select_fusion
  9.3 155.4 %all-gather.3.cloned.1.call-done = bf16[3072,2048]{1,0:T(8,128)(2,1)} async-done(((bf16[384,2048]{1,0:T(8,128)(2,1)}), bf16[3072,2048]{1,0:T(8,128)(2,1)}) %all-gather.3.cloned.1.call-update) | async-done | bytes 12582928 | tf_op jit(solution)/shard_map/all_gather | solution.py:17
  164.6 9.2 %reduce_sum.50 = bf16[384,2048]{1,0:T(8,128)(2,1)} reduce(bf16[8,384,2048]{2,1,0:T(8,128)(2,1)} %bitcast.257, bf16[]{:T(256)} %constant.52.clone.1), dimensions={0}, to_apply=%region_0.1 | reduce | flops 5505024 | bytes 14155778 | tf_op jit(solution)/shard_map/reduce_sum | solution.py:17
  173.8 3.6 collective-permute-start
  177.4 2.1 collective-permute-start.1
  179.6 2.5 copy.74
  182.3 4.4 copy.75
  186.9 2.0 and_and_fusion
  188.9 24.5 %collective-permute-done = bf16[384,2048]{1,0:T(8,128)(2,1)} collective-permute-done((bf16[384,2048]{1,0:T(8,128)(2,1)}, bf16[384,2048]{1,0:T(8,128)(2,1)}, u32[]{:S(2)}, u32[]{:S(2)}) %collective-permute-start) | collective-permute-done | bytes 1572896 | tf_op jit(solution)/shard_map/ppermute | solution.py:23
  213.4 15.0 %collective-permute-done.1 = bf16[384,2048]{1,0:T(8,128)(2,1)} collective-permute-done((bf16[384,2048]{1,0:T(8,128)(2,1)}, bf16[384,2048]{1,0:T(8,128)(2,1)}, u32[]{:S(2)}, u32[]{:S(2)}) %collective-permute-start.1) | collective-permute-done | bytes 1572896 | tf_op jit(solution)/shard_map/ppermute | solution.py:23
  228.4 2.1 pad_maximum_fusion
  231.4 1.9 copy.106
  233.3 2.6 copy.73
  235.9 223.8 %while.12 = (s32[]{:T(128)}, f32[8,1152,128]{2,1,0:T(8,128)}, f32[8,1152,128]{2,1,0:T(8,128)}, pred[384,1152]{0,1:T(8,128)(4,1)}, s32[8]{0:T(128)S(1)}, /*index=...) while((s32[]{:T(128)}, f32[8,1152,128]{2,1,0:T(8,128)}, ...), condition=%wide.region_10.11_spmd, body=%wide.region_4.10_spmd.sunk | while | flops 1720070784 | bytes 68940056 | solution.py:125
  244.9 3.7 fusion.120
  252.7 1.9 fusion.122
  254.6 2.2 fusion.125
  256.9 2.4 fusion.124
  259.3 2.2 fusion.123
  272.9 3.7 fusion.120
  280.7 1.9 fusion.122
  282.6 2.2 fusion.125
  284.9 2.4 fusion.124
  287.2 2.2 fusion.123
  300.9 3.7 fusion.120
  308.7 1.9 fusion.122
  310.6 2.2 fusion.125
  312.8 2.4 fusion.124
  315.2 2.2 fusion.123
  328.9 3.7 fusion.120
  336.7 1.9 fusion.122
  338.6 2.2 fusion.125
  340.9 2.4 fusion.124
  343.2 2.2 fusion.123
  356.9 3.7 fusion.120
  364.7 1.9 fusion.122
  366.6 2.2 fusion.125
  368.8 2.4 fusion.124
  371.2 2.2 fusion.123
  384.9 3.7 fusion.120
  392.7 1.9 fusion.122
  394.5 2.2 fusion.125
  396.8 2.4 fusion.124
  399.2 2.2 fusion.123
  412.8 3.7 fusion.120
  420.6 1.9 fusion.122
  422.5 2.2 fusion.125
  424.8 2.4 fusion.124
  427.2 2.2 fusion.123
  437.0 1.5 fusion.117
  440.8 3.7 fusion.120
  448.6 1.9 fusion.122
  450.5 2.2 fusion.125
  452.8 2.4 fusion.124
  455.2 2.2 fusion.123
  459.7 8.7 %copy_bitcast_fusion = (f32[1152,1024]{1,0:T(8,128)}, f32[1152,1024]{1,0:T(8,128)}) fusion(f32[8,1152,128]{2,1,0:T(8,128)} %get-tuple-element.53, f32[8,1152,128]{2,1,0:T(8,128)} %get-tuple-element.54), kind=kLoop, calls=%fused_computation.83 | loop fusion | bytes 18874368 | tf_op jit(solution)/shard_map/reshape | solution.py:128
  468.4 4.9 maximum_multiply_fusion
  474.0 1.9 collective-permute-start.2
  476.0 1.9 collective-permute-start.3
  477.9 64.8 %collective-permute-done.2 = f32[384,2048]{1,0:T(8,128)S(1)} collective-permute-done((f32[384,2048]{1,0:T(8,128)S(1)}, f32[384,2048]{1,0:T(8,128)S(1)}, u32[]{:S(2)}, u32[]{:S(2)}) %collective-permute-start.2) | collective-permute-done | bytes 3145760 | tf_op jit(solution)/shard_map/ppermute | solution.py:23
  542.7 37.5 %collective-permute-done.3 = f32[384,2048]{1,0:T(8,128)S(1)} collective-permute-done((f32[384,2048]{1,0:T(8,128)S(1)}, f32[384,2048]{1,0:T(8,128)S(1)}, u32[]{:S(2)}, u32[]{:S(2)}) %collective-permute-start.3) | collective-permute-done | bytes 3145760 | tf_op jit(solution)/shard_map/ppermute | solution.py:23
  580.1 2.7 fusion.63
  582.8 102.8 %all-reduce.2.cloned.1.call-done = f32[384,2048]{1,0:T(8,128)} async-done(((f32[384,2048]{1,0:T(8,128)}), f32[384,2048]{1,0:T(8,128)}) %all-reduce.2.cloned.1.call-update) | async-done | bytes 3145744 | tf_op jit(solution)/shard_map/psum | solution.py:135
  685.7 3.9 copy.121
  (174 shorter events, 108.6 us)
Async XLA Ops:
  6.5 158.1 %all-gather.3.cloned.1.call-start = ((), (), s32[]{:S(2)}) async-start(), calls=%async_computation.1 | async-start | bytes 14155776 | tf_op jit(solution)/shard_map/all_gather | solution.py:17
  9.2 676.5 %all-reduce.2.cloned.1.call-start = ((), (), s32[]{:S(2)}) async-start(), calls=%async_computation | async-start | bytes 6291456 | tf_op jit(solution)/shard_map/psum | solution.py:135
  164.6 14.9 %copy-start.2 = (bf16[1,384,3072]{2,1,0:T(8,128)(2,1)S(1)}, bf16[1,384,3072]{2,1,0:T(8,128)(2,1)}, u32[]{:S(2)}) copy-start(bf16[1,384,3072]{2,1,0:T(8,128)(2,1)} %param.5) | copy-start | bytes 7077892
  173.8 8.2 %copy-start.4 = (s32[31]{0:T(128)S(1)}, s32[31]{0:T(128)}, u32[]{:S(2)}) copy-start(s32[31]{0:T(128)} %param.7) | copy-start | bytes 376
  173.8 39.6 %collective-permute-start = (bf16[384,2048]{1,0:T(8,128)(2,1)}, bf16[384,2048]{1,0:T(8,128)(2,1)}, u32[]{:S(2)}, u32[]{:S(2)}) collective-permute-start(bf16[384,2048]{1,0:T(8,128)(2,1)} %reduce_sum.50), channel_id=1, source_target_pairs={{0,2},{1,3},{2,4},{3,5},{4,6},{5,7},{6,8},{7,9},{8,10},{9,11},{10,... | collective-permute-start | bytes 4718600 | tf_op jit(solution)/shard_map/ppermute | solution.py:23
  177.4 51.0 %collective-permute-start.1 = (bf16[384,2048]{1,0:T(8,128)(2,1)}, bf16[384,2048]{1,0:T(8,128)(2,1)}, u32[]{:S(2)}, u32[]{:S(2)}) collective-permute-start(bf16[384,2048]{1,0:T(8,128)(2,1)} %reduce_sum.50), channel_id=1, source_target_pairs={{0,1},{1,2},{2,3},{3,4},{4,5},{5,6},{6,7},{7,8},{8,9},{9,10},{10,1... | collective-permute-start | bytes 4718600 | tf_op jit(solution)/shard_map/ppermute | solution.py:23
  182.0 46.4 %copy-start.3 = (bf16[384,2048]{1,0:T(8,128)(2,1)S(1)}, bf16[384,2048]{1,0:T(8,128)(2,1)}, u32[]{:S(2)}) copy-start(bf16[384,2048]{1,0:T(8,128)(2,1)} %reduce_sum.50) | copy-start | bytes 4718596
  248.6 1.5 copy-start
  256.9 4.6 copy-start.1
  276.6 1.5 copy-start
  284.8 4.6 copy-start.1
  304.6 1.5 copy-start
  312.8 4.6 copy-start.1
  332.6 1.5 copy-start
  340.8 4.6 copy-start.1
  360.6 1.5 copy-start
  368.8 4.6 copy-start.1
  388.6 1.5 copy-start
  396.8 4.6 copy-start.1
  416.5 1.5 copy-start
  424.8 4.6 copy-start.1
  444.5 1.5 copy-start
  452.8 4.6 copy-start.1
  474.0 68.7 %collective-permute-start.2 = (f32[384,2048]{1,0:T(8,128)S(1)}, f32[384,2048]{1,0:T(8,128)S(1)}, u32[]{:S(2)}, u32[]{:S(2)}) collective-permute-start(f32[384,2048]{1,0:T(8,128)S(1)} %get-tuple-element.122), channel_id=1, source_target_pairs={{1,0},{2,1},{3,2},{4,3},{5,4},{6,5},{7,6},{8,7},{9,8},{10,9},{11,1... | collective-permute-start | bytes 9437192 | tf_op jit(solution)/shard_map/ppermute | solution.py:23
  476.0 104.2 %collective-permute-start.3 = (f32[384,2048]{1,0:T(8,128)S(1)}, f32[384,2048]{1,0:T(8,128)S(1)}, u32[]{:S(2)}, u32[]{:S(2)}) collective-permute-start(f32[384,2048]{1,0:T(8,128)S(1)} %get-tuple-element.123), channel_id=1, source_target_pairs={{2,0},{3,1},{4,2},{5,3},{6,4},{7,5},{8,6},{9,7},{10,8},{11,9},{12,... | collective-permute-start | bytes 9437192 | tf_op jit(solution)/shard_map/ppermute | solution.py:23
Sparse Core Ops, SparseCore 0:
  9.9 154.6 all-gather.2
  583.0 102.6 all-reduce.1
